TPU v7x, 32 devices: a whole 2x2x4 slice. The times are simulated.
32 devices in a mesh: grp: 4 (over y, x), sub: 8 (over z, core).
Axes of the slice: x: 2, y: 2, z: 4, core: 2. Of those that a mesh axis runs over, the one named last changes fastest.
Arguments:
- right_side: float32 [24576, 160], P(('grp', 'sub')), may hold values from -6 to 6
- iterate_in: float32 [24576, 160], P(('grp', 'sub')), may hold values from -6 to 6
- diagonal: float32 [24576], P(('grp', 'sub')), may hold values from 1.5 to 4
- block_values: bfloat16 [32, 6, 3, 128, 128], P(('grp', 'sub')), may hold values from -0.125 to 0.125
- block_cols: int32 [32, 6, 3], P(('grp', 'sub')), may hold values from 0 to 5, as said below
- couple_left: bfloat16 [24576, 128], P(('grp', 'sub')), may hold values from -0.125 to 0.125
- couple_right: bfloat16 [24576, 128], P(('grp', 'sub')), may hold values from -0.125 to 0.125
- send_rows: int32 [32, 2, 128], P(('grp', 'sub')), may hold values from 0 to 767, as said below
- local_inverse: bfloat16 [32, 1024, 1024], P(('grp', 'sub')), may hold values from -0.3 to 2.3, as said below
- coarse_basis: bfloat16 [32, 1024, 32], P(('grp', 'sub')), may hold values from -0.1875 to 0.1875
- coarse_diag: float32 [32, 32, 32], P(('grp', 'sub')), may hold values from -54 to 59.5, as said below
- coarse_up: float32 [32, 32, 32], P(('grp', 'sub')), may hold values from -29.7 to 27
Outputs:
- iterate: float32 [24576, 160], P(('grp', 'sub'))
- residual: float32 [24576, 160], P(('grp', 'sub'))
Inputs may be any that keep to these rules, and one draw needn't show every extreme that they name: `block_cols`: the 3 column blocks of one row block are distinct. `send_rows`: the 256 rows listed for one subdomain are distinct. `local_inverse`: each block is symmetric positive definite. `coarse_diag`: each block is symmetric; with coarse_up the coarse operator is symmetric positive definite.
All inputs are finite; a program needn't handle non-finite values.
Results may differ from a plain program's by a relative error of at most 0.0032.
Values may be sent and summed in bfloat16 or wider, within the bound.
No kernel may reach another device: no remote copies, remote signals or barrier semaphores. Data moves between devices by JAX's collectives and lax.ppermute only.
A program may use at most 64 MiB of HBM per device.

v0:
```python
import jax
import jax.numpy as jnp
from jax import lax
from jax.sharding import PartitionSpec as P


def with_halo(cells, sides, width):
    for axis, dim in sides:
        count = lax.axis_size(axis)
        ends = count - 1
        head = lax.slice_in_dim(cells, 0, width, axis=dim)
        tail = lax.slice_in_dim(cells, cells.shape[dim] - width, cells.shape[dim], axis=dim)
        cells = jnp.concatenate(
            [
                lax.ppermute(tail, axis, [(i, (i + 1) % count) for i in range(ends)]),
                cells,
                lax.ppermute(head, axis, [((i + 1) % count, i) for i in range(ends)]),
            ],
            axis=dim,
        )
    return cells


def chol_solve(factor, values):
    halfway = lax.linalg.triangular_solve(factor, values, left_side=True, lower=True)
    return lax.linalg.triangular_solve(
        factor, halfway, left_side=True, lower=True, transpose_a=True
    )


def solve_chain(diagonal_blocks, upper, values):
    highest = lax.Precision.HIGHEST
    blocks_total = diagonal_blocks.shape[0]
    padded_total = 1
    while padded_total < blocks_total:
        padded_total = padded_total * 2
    extra = padded_total - blocks_total
    block_width = diagonal_blocks.shape[1]
    identity = jnp.eye(block_width, dtype=jnp.float32)
    diag_now = jnp.concatenate(
        [diagonal_blocks, jnp.broadcast_to(identity, (extra, block_width, block_width))], axis=0
    )
    upper_now = jnp.concatenate(
        [upper[:-1], jnp.zeros((extra + 1, block_width, block_width), jnp.float32)], axis=0
    )
    rhs_now = jnp.concatenate([values, jnp.zeros((extra,) + values.shape[1:], jnp.float32)], axis=0)
    levels = []
    while diag_now.shape[0] > 1:
        diag_even = diag_now[0::2]
        diag_odd = diag_now[1::2]
        upper_even = upper_now[0::2]
        upper_odd = upper_now[1::2]
        rhs_even = rhs_now[0::2]
        rhs_odd = rhs_now[1::2]
        factor = jnp.linalg.cholesky(diag_odd)
        stacked = jnp.concatenate([jnp.swapaxes(upper_even, 1, 2), upper_odd, rhs_odd], axis=2)
        through = chol_solve(factor, stacked)
        toward_left = through[:, :, :block_width]
        toward_right = through[:, :, block_width : 2 * block_width]
        odd_loads = through[:, :, 2 * block_width :]
        new_diag = diag_even - jnp.einsum(
            "mab,mbc->mac", upper_even, toward_left, precision=highest
        )
        new_upper = -jnp.einsum("mab,mbc->mac", upper_even, toward_right, precision=highest)
        new_rhs = rhs_even - jnp.einsum("mab,mbn->man", upper_even, odd_loads, precision=highest)
        from_diag = jnp.einsum("mba,mbc->mac", upper_odd, toward_right, precision=highest)
        from_rhs = jnp.einsum("mba,mbn->man", upper_odd, odd_loads, precision=highest)
        new_diag = new_diag - jnp.concatenate(
            [jnp.zeros_like(from_diag[:1]), from_diag[:-1]], axis=0
        )
        new_rhs = new_rhs - jnp.concatenate([jnp.zeros_like(from_rhs[:1]), from_rhs[:-1]], axis=0)
        levels.append((toward_left, toward_right, odd_loads))
        diag_now, upper_now, rhs_now = (new_diag, new_upper, new_rhs)
    solution = chol_solve(jnp.linalg.cholesky(diag_now[0]), rhs_now[0])[None]
    for toward_left, toward_right, odd_loads in reversed(levels):
        next_sol = jnp.concatenate([solution[1:], jnp.zeros_like(solution[:1])], axis=0)
        odd_part = (
            odd_loads
            - jnp.einsum("mab,mbn->man", toward_left, solution, precision=highest)
            - jnp.einsum("mab,mbn->man", toward_right, next_sol, precision=highest)
        )
        solution = jnp.stack([solution, odd_part], axis=1).reshape((-1,) + solution.shape[1:])
    return solution[:blocks_total]


def shards(
    right_side,
    iterate_in,
    diagonal,
    block_values,
    block_cols,
    couple_left,
    couple_right,
    send_rows,
    local_inverse,
    coarse_basis,
    coarse_diag,
    coarse_up,
):
    bf16 = jnp.bfloat16
    f32 = jnp.float32
    highest = lax.Precision.HIGHEST
    intersection = send_rows.shape[2]
    rows_own = right_side.shape[0]
    cases = right_side.shape[1]
    row_blocks = block_cols.shape[1]
    modes = coarse_basis.shape[2]
    column_blocks = block_cols[0]
    sent_left_rows = send_rows[0, 0]
    sent_right_rows = send_rows[0, 1]

    def neighbour_rows(source):
        boundary = jnp.stack([source[sent_left_rows], source[sent_right_rows]])
        padded = with_halo(boundary, ((("grp", "sub"), 0),), 1)
        return (padded[0], padded[3])

    def apply_operator(vector):
        rounded = vector.astype(bf16)
        from_left, from_right = neighbour_rows(rounded)
        blocks = rounded.reshape(row_blocks, -1, cases)
        picked = blocks[column_blocks]
        sparse = jnp.einsum(
            "itab,itbn->ian", block_values[0], picked, preferred_element_type=f32
        ).reshape(rows_own, cases)
        coupled = jnp.dot(couple_left, from_left, preferred_element_type=f32) + jnp.dot(
            couple_right, from_right, preferred_element_type=f32
        )
        return diagonal[:, None] * vector + (sparse + coupled)

    residual_start = right_side - apply_operator(iterate_in)
    rounded = residual_start.astype(bf16)
    from_left, from_right = neighbour_rows(rounded)
    extended = jnp.concatenate([from_left, rounded, from_right], axis=0)
    local_part = jnp.dot(local_inverse[0], extended, preferred_element_type=f32)
    coarse_in = jnp.dot(coarse_basis[0].T, extended, preferred_element_type=f32)
    blocks_diag = lax.all_gather(coarse_diag, "sub", axis=0, tiled=True)
    blocks_up = lax.all_gather(coarse_up, "sub", axis=0, tiled=True)
    group = lax.axis_index("grp")
    groups = lax.axis_size("grp")
    member = lax.axis_index("sub")
    members = lax.axis_size("sub")
    keep = (group < groups - 1).astype(f32)
    first_up = blocks_up[0]
    last_up = blocks_up[members - 1] * keep
    columns = lax.all_gather(coarse_in[None], "sub", axis=0, tiled=True)
    width = columns.shape[2]
    inner_count = members - 1
    empty_cols = jnp.zeros((inner_count, modes, modes), f32)
    left_cols = empty_cols.at[0].set(first_up.T)
    right_cols = empty_cols.at[inner_count - 1].set(last_up)
    stacked = jnp.concatenate([columns[1:], left_cols, right_cols], axis=2)
    solved = solve_chain(blocks_diag[1:], blocks_up[1:], stacked)
    sol_loads = solved[:, :, :width]
    sol_left = solved[:, :, width : width + modes]
    sol_right = solved[:, :, width + modes :]
    self_left = jnp.dot(first_up, sol_left[0], precision=highest)
    cross_term = jnp.dot(first_up, sol_right[0], precision=highest)
    rhs_first = jnp.dot(first_up, sol_loads[0], precision=highest)
    self_right = jnp.dot(last_up.T, sol_right[-1], precision=highest)
    rhs_last = jnp.dot(last_up.T, sol_loads[-1], precision=highest)
    sep_diag = lax.all_gather(blocks_diag[0][None], "grp", axis=0, tiled=True)
    sep_rhs = lax.all_gather(columns[0][None], "grp", axis=0, tiled=True)
    all_left = lax.all_gather(self_left[None], "grp", axis=0, tiled=True)
    all_right = lax.all_gather(self_right[None], "grp", axis=0, tiled=True)
    all_cross = lax.all_gather(cross_term[None], "grp", axis=0, tiled=True)
    all_first = lax.all_gather(rhs_first[None], "grp", axis=0, tiled=True)
    all_last = lax.all_gather(rhs_last[None], "grp", axis=0, tiled=True)
    prev_right = jnp.concatenate([jnp.zeros_like(all_right[:1]), all_right[:-1]], axis=0)
    prev_last = jnp.concatenate([jnp.zeros_like(all_last[:1]), all_last[:-1]], axis=0)
    reduced_diag = sep_diag - all_left - prev_right
    reduced_rhs = sep_rhs - all_first - prev_last
    sep_sol = solve_chain(reduced_diag, -all_cross, reduced_rhs)
    padded_sol = jnp.concatenate([sep_sol, jnp.zeros_like(sep_sol[:1])], axis=0)
    mine = lax.dynamic_index_in_dim(padded_sol, group, 0, keepdims=False)
    after = lax.dynamic_index_in_dim(padded_sol, group + 1, 0, keepdims=False)
    inner_sol = (
        sol_loads
        - jnp.einsum("ivw,wn->ivn", sol_left, mine, precision=highest)
        - jnp.einsum("ivw,wn->ivn", sol_right, after, precision=highest)
    )
    group_sol = jnp.concatenate([mine[None], inner_sol], axis=0)
    coarse_sol = lax.dynamic_index_in_dim(group_sol, member, 0, keepdims=False)
    correction = local_part + jnp.dot(
        coarse_basis[0], coarse_sol.astype(bf16), preferred_element_type=f32
    )
    tails = jnp.stack([correction[:intersection], correction[intersection + rows_own :]])
    returned = with_halo(tails.astype(jnp.bfloat16), ((("grp", "sub"), 0),), 1).astype(tails.dtype)
    owned = correction[intersection : intersection + rows_own]
    owned = owned.at[sent_right_rows].add(returned[3])
    owned = owned.at[sent_left_rows].add(returned[0])
    inner = lax.psum(jnp.sum(residual_start * owned, axis=0), ("grp", "sub"))
    image = apply_operator(owned)
    curvature = lax.psum(jnp.sum(owned * image, axis=0), ("grp", "sub"))
    step_size = inner / curvature
    return (iterate_in + step_size * owned, residual_start - step_size * image)


def solution(mesh):
    in_specs = (
        P(("grp", "sub"), None),
        P(("grp", "sub"), None),
        P(("grp", "sub")),
        P(("grp", "sub"), None, None, None, None),
        P(("grp", "sub"), None, None),
        P(("grp", "sub"), None),
        P(("grp", "sub"), None),
        P(("grp", "sub"), None, None),
        P(("grp", "sub"), None, None),
        P(("grp", "sub"), None, None),
        P(("grp", "sub"), None, None),
        P(("grp", "sub"), None, None),
    )
    out_specs = (P(("grp", "sub"), None), P(("grp", "sub"), None))
    return jax.shard_map(shards, mesh=mesh, in_specs=in_specs, out_specs=out_specs, check_vma=False)
```

profile of v0, /device:TPU:14, one launch (start us, length us, event | category | flops | bytes accessed | tf_op | source)
XLA Modules:
  0.0 289.2 jit_solution(11546375033526299166)
XLA Ops:
  7.7 2.4 collective-permute-start
  10.4 14.8 %all_gather.32 = f32[8,32,32]{2,1,0:T(8,128)S(1)} all-gather(f32[1,32,32]{2,1,0:T(8,128)S(1)} %copy-done.34), channel_id=1, replica_groups=mesh['grp'=4,'sub'=8] {'sub'}, dimensions={0}, use_global_device_ids=true | all-gather | bytes 36864 | tf_op jit(solution)/shard_map/all_gather | solution.py:137
  25.2 14.0 %all_gather.30 = f32[8,32,32]{2,1,0:T(8,128)S(1)} all-gather(f32[1,32,32]{2,1,0:T(8,128)S(1)} %copy-done.35), channel_id=1, replica_groups=mesh['grp'=4,'sub'=8] {'sub'}, dimensions={0}, use_global_device_ids=true | all-gather | bytes 36864 | tf_op jit(solution)/shard_map/all_gather | solution.py:136
  39.5 11.7 %custom-call.47 = f32[4,32,32]{2,1,0:T(8,128)S(1)} custom-call(f32[4,32,32]{2,1,0:T(8,128)S(1)} %copy.185), custom_call_target="Cholesky" | custom-call | tf_op jit(solution)/shard_map/jit(cholesky)/cholesky | solution.py:55
  61.8 4.0 %collective-permute-start.3 = (bf16[1,128,160]{1,2,0:T(8,128)(2,1)S(1)}, bf16[1,128,160]{1,2,0:T(8,128)(2,1)S(1)}, u32[]{:S(2)}, u32[]{:S(2)}) collective-permute-start(bf16[1,128,160]{1,2,0:T(8,128)(2,1)S(1)} %bitcast.412), channel_id=1, source_target_pairs={{1,0},{2,1},{3,2},{4,3},{5,4},{6,5},{7,6},{8,7},{9,8},{10,9},{11,1... | collective-permute-start | bytes 122888 | tf_op jit(solution)/shard_map/ppermute | solution.py:17
  68.7 11.2 %custom-call.48 = f32[4,1,32,32]{2,3,1,0:T(8,128)} custom-call(f32[4,1,32,32]{3,2,1,0:T(8,128)} %select_bitcast_fusion), custom_call_target="InvertDiagBlocksLowerTriangular" | custom-call | tf_op jit(solution)/shard_map/triangular_solve | solution.py:26
  79.9 9.1 %all_gather.31 = f32[4,32,32]{2,1,0:T(8,128)S(1)} all-gather(f32[1,32,32]{2,1,0:T(8,128)S(1)} %slice-done.1), channel_id=1, replica_groups=mesh['grp'=4,'sub'=8] {'grp'}, dimensions={0}, use_global_device_ids=true | all-gather | bytes 20480 | tf_op jit(solution)/shard_map/all_gather | solution.py:161
  90.5 12.7 %all-gather = f32[256,160]{1,0:T(8,128)S(1)} all-gather(f32[32,160]{1,0:T(8,128)S(1)} %convolution_bitcast_fusion.11), channel_id=2, replica_groups=mesh['grp'=4,'sub'=8] {'sub'}, dimensions={0}, use_global_device_ids=true | all-gather | bytes 184320 | tf_op jit(solution)/shard_map/all_gather | solution.py:145
  106.0 5.9 %custom-call.57 = f32[2,32,32]{2,1,0:T(8,128)S(1)} custom-call(f32[2,32,32]{2,1,0:T(8,128)S(1)} %fusion.117), custom_call_target="Cholesky" | custom-call | tf_op jit(solution)/shard_map/jit(cholesky)/cholesky | solution.py:55
  112.1 4.9 %custom-call.49 = f32[2,1,32,32]{2,3,1,0:T(8,128)S(1)} custom-call(f32[2,1,32,32]{3,2,1,0:T(8,128)S(1)} %fusion.119), custom_call_target="InvertDiagBlocksLowerTriangular" | custom-call | tf_op jit(solution)/shard_map/triangular_solve | solution.py:26
  119.1 2.9 %custom-call.58 = f32[1,32,32]{2,1,0:T(8,128)S(1)} custom-call(f32[1,32,32]{2,1,0:T(8,128)S(1)} %fusion.169), custom_call_target="Cholesky" | custom-call | tf_op jit(solution)/shard_map/jit(cholesky)/cholesky | solution.py:55
  123.2 2.4 custom-call.50
  126.9 2.9 %cholesky.184 = f32[32,32]{1,0:T(8,128)S(1)} custom-call(f32[32,32]{1,0:T(8,128)S(1)} %fusion.150), custom_call_target="Cholesky" | custom-call | tf_op jit(solution)/shard_map/jit(cholesky)/cholesky | solution.py:74
  131.1 2.4 custom-call.51
  136.5 7.0 %all-gather.6 = f32[128,160]{1,0:T(8,128)S(1)} all-gather(f32[32,160]{1,0:T(8,128)S(1)} %slice-done), channel_id=8, replica_groups=mesh['grp'=4,'sub'=8] {'grp'}, dimensions={0}, use_global_device_ids=true | all-gather | bytes 102400 | tf_op jit(solution)/shard_map/all_gather | solution.py:162
  143.4 8.9 %all-gather.4 = f32[128,160]{1,0:T(8,128)S(1)} all-gather(f32[32,160]{1,0:T(8,128)S(1)} %convolution_bitcast_fusion.7), channel_id=6, replica_groups=mesh['grp'=4,'sub'=8] {'grp'}, dimensions={0}, use_global_device_ids=true | all-gather | bytes 102400 | tf_op jit(solution)/shard_map/all_gather | solution.py:166
  152.4 7.1 %all-gather.5 = f32[128,160]{1,0:T(8,128)S(1)} all-gather(f32[32,160]{1,0:T(8,128)S(1)} %fusion.101), channel_id=7, replica_groups=mesh['grp'=4,'sub'=8] {'grp'}, dimensions={0}, use_global_device_ids=true | all-gather | bytes 102400 | tf_op jit(solution)/shard_map/all_gather | solution.py:167
  159.6 8.7 %all-gather.3 = f32[128,32]{1,0:T(8,128)S(1)} all-gather(f32[32,32]{1,0:T(8,128)S(1)} %copy.214), channel_id=5, replica_groups=mesh['grp'=4,'sub'=8] {'grp'}, dimensions={0}, use_global_device_ids=true | all-gather | bytes 20480 | tf_op jit(solution)/shard_map/all_gather | solution.py:165
  168.5 6.7 %all-gather.2 = f32[128,32]{1,0:T(8,128)S(1)} all-gather(f32[32,32]{1,0:T(8,128)S(1)} %fusion.145), channel_id=4, replica_groups=mesh['grp'=4,'sub'=8] {'grp'}, dimensions={0}, use_global_device_ids=true | all-gather | bytes 20480 | tf_op jit(solution)/shard_map/all_gather | solution.py:164
  175.4 8.9 %all-gather.1 = f32[128,32]{1,0:T(8,128)S(1)} all-gather(f32[32,32]{1,0:T(8,128)S(1)} %copy.208), channel_id=3, replica_groups=mesh['grp'=4,'sub'=8] {'grp'}, dimensions={0}, use_global_device_ids=true | all-gather | bytes 20480 | tf_op jit(solution)/shard_map/all_gather | solution.py:163
  184.6 5.9 %custom-call.59 = f32[2,32,32]{2,1,0:T(8,128)S(1)} custom-call(f32[2,32,32]{2,1,0:T(8,128)S(1)} %fusion.112), custom_call_target="Cholesky" | custom-call | tf_op jit(solution)/shard_map/jit(cholesky)/cholesky | solution.py:55
  190.7 4.9 %custom-call.52 = f32[2,1,32,32]{2,3,1,0:T(8,128)S(1)} custom-call(f32[2,1,32,32]{3,2,1,0:T(8,128)S(1)} %fusion.118), custom_call_target="InvertDiagBlocksLowerTriangular" | custom-call | tf_op jit(solution)/shard_map/triangular_solve | solution.py:26
  197.6 2.9 %custom-call.60 = f32[1,32,32]{2,1,0:T(8,128)S(1)} custom-call(f32[1,32,32]{2,1,0:T(8,128)S(1)} %fusion.158), custom_call_target="Cholesky" | custom-call | tf_op jit(solution)/shard_map/jit(cholesky)/cholesky | solution.py:55
  201.9 2.4 custom-call.53
  205.5 2.9 %cholesky.216 = f32[32,32]{1,0:T(8,128)S(1)} custom-call(f32[32,32]{1,0:T(8,128)S(1)} %fusion.149), custom_call_target="Cholesky" | custom-call | tf_op jit(solution)/shard_map/jit(cholesky)/cholesky | solution.py:74
  209.8 2.4 custom-call.54
  217.3 2.4 collective-permute-start.4
  220.1 4.3 %collective-permute-done.4 = bf16[1,128,160]{1,2,0:T(8,128)(2,1)S(1)} collective-permute-done((bf16[1,128,160]{1,2,0:T(8,128)(2,1)S(1)}, bf16[1,128,160]{1,2,0:T(8,128)(2,1)S(1)}, u32[]{:S(2)}, u32[]{:S(2)}) %collective-permute-start.4) | collective-permute-done | bytes 40992 | tf_op jit(solution)/shard_map/ppermute | solution.py:15
  233.4 2.4 collective-permute-start.6
  238.6 3.1 %collective-permute-done.6 = bf16[1,128,160]{2,1,0:T(8,128)(2,1)S(1)} collective-permute-done((bf16[1,128,160]{2,1,0:T(8,128)(2,1)S(1)}, bf16[1,128,160]{2,1,0:T(8,128)(2,1)S(1)}, u32[]{:S(2)}, u32[]{:S(2)}) %collective-permute-start.6) | collective-permute-done | bytes 40992 | tf_op jit(solution)/shard_map/ppermute | solution.py:15
  242.8 44.1 %all-reduce.16 = (f32[160]{0:T(256)S(1)}, f32[160]{0:T(256)S(1)}) all-reduce(f32[160]{0:T(256)S(1)} %get-tuple-element.30, f32[160]{0:T(256)S(1)} %get-tuple-element.29), channel_id=1, replica_groups=mesh['grp'=4,'sub'=8] {'grp','sub'}, use_global_device_ids=true, to_apply=%region_11.15 | all-reduce | flops 320 | bytes 2560 | tf_op jit(solution)/shard_map/psum | solution.py:191
  286.9 2.3 multiply_subtract_fusion
  (282 shorter events, 58.2 us)
Async XLA Ops:
  0.6 213.9 %copy-start = (bf16[1,1024,1024]{2,1,0:T(8,128)(2,1)S(1)}, bf16[1,1024,1024]{2,1,0:T(8,128)(2,1)}, u32[]{:S(2)}) copy-start(bf16[1,1024,1024]{2,1,0:T(8,128)(2,1)} %param.27) | copy-start | bytes 6291460
  0.6 9.5 %copy-start.43 = (s32[1,6,3]{1,0,2:T(1,128)S(1)}, s32[1,6,3]{1,0,2:T(1,128)}, u32[]{:S(2)}) copy-start(s32[1,6,3]{1,0,2:T(1,128)} %param.23) | copy-start | bytes 220
  0.7 9.7 %copy-start.34 = (f32[1,32,32]{2,1,0:T(8,128)S(1)}, f32[1,32,32]{2,1,0:T(8,128)}, u32[]{:S(2)}) copy-start(f32[1,32,32]{2,1,0:T(8,128)} %param.30) | copy-start | bytes 12292
  0.7 24.5 %copy-start.35 = (f32[1,32,32]{2,1,0:T(8,128)S(1)}, f32[1,32,32]{2,1,0:T(8,128)}, u32[]{:S(2)}) copy-start(f32[1,32,32]{2,1,0:T(8,128)} %param.29) | copy-start | bytes 12292
  2.8 7.3 %copy-start.38 = (s32[128]{0:T(128)}, s32[128]{0:T(128)S(1)}, u32[]{:S(2)}) copy-start(s32[128]{0:T(128)S(1)} %get-tuple-element.52) | copy-start | bytes 1540
  2.8 22.4 %copy-start.40 = (s32[128]{0:T(128)}, s32[128]{0:T(128)S(1)}, u32[]{:S(2)}) copy-start(s32[128]{0:T(128)S(1)} %get-tuple-element.51) | copy-start | bytes 1540
  2.8 22.4 %copy-start.36 = (s32[1024]{0:T(1024)}, s32[1024]{0:T(1024)S(1)}, u32[]{:S(2)}) copy-start(s32[1024]{0:T(1024)S(1)} %get-tuple-element.59) | copy-start | bytes 12292
  2.8 22.4 %copy-start.37 = (s32[1024]{0:T(1024)}, s32[1024]{0:T(1024)S(1)}, u32[]{:S(2)}) copy-start(s32[1024]{0:T(1024)S(1)} %get-tuple-element.58) | copy-start | bytes 12292
  4.3 52.1 %collective-permute-start.1 = (bf16[1,128,160]{2,1,0:T(8,128)(2,1)}, bf16[1,128,160]{2,1,0:T(8,128)(2,1)}, u32[]{:S(2)}, u32[]{:S(2)}) collective-permute-start(bf16[1,128,160]{2,1,0:T(8,128)(2,1)} %bitcast.13), channel_id=1, source_target_pairs={{1,0},{2,1},{3,2},{4,3},{5,4},{6,5},{7,6},{8,7},{9,8},{10,9},{11,1... | collective-permute-start | bytes 122888 | tf_op jit(solution)/shard_map/ppermute | solution.py:17
  7.7 49.8 %collective-permute-start = (bf16[1,128,160]{2,1,0:T(8,128)(2,1)}, bf16[1,128,160]{2,1,0:T(8,128)(2,1)}, u32[]{:S(2)}, u32[]{:S(2)}) collective-permute-start(bf16[1,128,160]{2,1,0:T(8,128)(2,1)} %bitcast.9), channel_id=1, source_target_pairs={{0,1},{1,2},{2,3},{3,4},{4,5},{5,6},{6,7},{7,8},{8,9},{9,10},{10,1... | collective-permute-start | bytes 122888 | tf_op jit(solution)/shard_map/ppermute | solution.py:15
  10.1 43.6 %copy-start.24 = (pred[32,32]{1,0:T(8,128)(4,1)}, pred[32,32]{1,0:T(8,128)(4,1)S(1)}, u32[]{:S(2)}) copy-start(pred[32,32]{1,0:T(8,128)(4,1)S(1)} %iota_compare_fusion.3) | copy-start | bytes 3076
  10.2 45.5 %copy-start.22 = (pred[32,32]{1,0:T(8,128)(4,1)}, pred[32,32]{1,0:T(8,128)(4,1)S(1)}, u32[]{:S(2)}) copy-start(pred[32,32]{1,0:T(8,128)(4,1)S(1)} %iota_compare_fusion.7) | copy-start | bytes 3076
  10.4 43.3 %copy-start.30 = (s32[1024]{0:T(1024)}, s32[1024]{0:T(1024)S(1)}, u32[]{:S(2)}) copy-start(s32[1024]{0:T(1024)S(1)} %pad_clamp_fusion.2) | copy-start | bytes 12292
  39.2 12.7 %copy-start.11 = (f32[8,32,32]{2,1,0:T(8,128)}, f32[8,32,32]{2,1,0:T(8,128)S(1)}, u32[]{:S(2)}) copy-start(f32[8,32,32]{2,1,0:T(8,128)S(1)} %all_gather.30) | copy-start | bytes 98308
  56.4 46.9 %copy-start.13 = (f32[1,32,32]{2,1,0:T(8,128)}, f32[1,32,32]{2,1,0:T(8,128)S(1)}, u32[]{:S(2)}) copy-start(f32[1,32,32]{2,1,0:T(8,128)S(1)} %get-tuple-element.38) | copy-start | bytes 12292
  59.5 20.4 %slice-start.1 = ((f32[8,32,32]{2,1,0:T(8,128)}), f32[1,32,32]{2,1,0:T(8,128)S(1)}, s32[]{:S(2)}) async-start(f32[8,32,32]{2,1,0:T(8,128)} %copy-done.11), calls=%async_computation.1 | async-start | bytes 32768 | tf_op jit(solution)/shard_map/slice | solution.py:161
  59.6 30.7 %copy-start.20 = (bf16[1,1024,32]{1,2,0:T(8,128)(2,1)S(1)}, bf16[1,1024,32]{1,2,0:T(8,128)(2,1)}, u32[]{:S(2)}) copy-start(bf16[1,1024,32]{1,2,0:T(8,128)(2,1)} %param.28) | copy-start | bytes 196612
  61.8 27.9 %collective-permute-start.3 = (bf16[1,128,160]{1,2,0:T(8,128)(2,1)S(1)}, bf16[1,128,160]{1,2,0:T(8,128)(2,1)S(1)}, u32[]{:S(2)}, u32[]{:S(2)}) collective-permute-start(bf16[1,128,160]{1,2,0:T(8,128)(2,1)S(1)} %bitcast.412), channel_id=1, source_target_pairs={{1,0},{2,1},{3,2},{4,3},{5,4},{6,5},{7,6},{8,7},{9,8},{10,9},{11,1... | collective-permute-start | bytes 122888 | tf_op jit(solution)/shard_map/ppermute | solution.py:17
  65.9 23.7 %collective-permute-start.2 = (bf16[1,128,160]{1,2,0:T(8,128)(2,1)S(1)}, bf16[1,128,160]{1,2,0:T(8,128)(2,1)S(1)}, u32[]{:S(2)}, u32[]{:S(2)}) collective-permute-start(bf16[1,128,160]{1,2,0:T(8,128)(2,1)S(1)} %bitcast.413), channel_id=1, source_target_pairs={{0,1},{1,2},{2,3},{3,4},{4,5},{5,6},{6,7},{7,8},{8,9},{9,10},{10,1... | collective-permute-start | bytes 122888 | tf_op jit(solution)/shard_map/ppermute | solution.py:15
  90.3 13.0 %copy-start.18 = (f32[4,1,32,32]{2,3,1,0:T(8,128)S(1)}, f32[4,1,32,32]{2,3,1,0:T(8,128)}, u32[]{:S(2)}) copy-start(f32[4,1,32,32]{2,3,1,0:T(8,128)} %custom-call.48) | copy-start | bytes 49156
  90.3 13.1 %copy-start.19 = (f32[4,32,32]{2,1,0:T(8,128)S(1)}, f32[4,32,32]{2,1,0:T(8,128)}, u32[]{:S(2)}) copy-start(f32[4,32,32]{2,1,0:T(8,128)} %copy.187) | copy-start | bytes 49156
  104.5 7.3 %copy-start.25 = (pred[32,32]{1,0:T(8,128)(4,1)S(1)}, pred[32,32]{1,0:T(8,128)(4,1)}, u32[]{:S(2)}) copy-start(pred[32,32]{1,0:T(8,128)(4,1)} %copy-done.24) | copy-start | bytes 3076
  104.5 7.5 %copy-start.23 = (pred[32,32]{1,0:T(8,128)(4,1)S(1)}, pred[32,32]{1,0:T(8,128)(4,1)}, u32[]{:S(2)}) copy-start(pred[32,32]{1,0:T(8,128)(4,1)} %copy-done.22) | copy-start | bytes 3076
  135.2 33.1 %copy-start.44 = (pred[4]{0:T(512)(128)(4,1)S(1)}, pred[4]{0:T(512)(128)(4,1)}, u32[]{:S(2)}) copy-start(pred[4]{0:T(512)(128)(4,1)} %constant.263.clone.1) | copy-start | bytes 16
  152.4 32.1 %copy-start.17 = (f32[4,32,32]{1,2,0:T(8,128)S(1)}, f32[4,32,32]{1,2,0:T(8,128)}, u32[]{:S(2)}) copy-start(f32[4,32,32]{1,2,0:T(8,128)} %copy.210) | copy-start | bytes 49156
  215.4 4.7 %collective-permute-start.5 = (bf16[1,128,160]{1,2,0:T(8,128)(2,1)S(1)}, bf16[1,128,160]{1,2,0:T(8,128)(2,1)S(1)}, u32[]{:S(2)}, u32[]{:S(2)}) collective-permute-start(bf16[1,128,160]{1,2,0:T(8,128)(2,1)S(1)} %get-tuple-element.34), channel_id=1, source_target_pairs={{1,0},{2,1},{3,2},{4,3},{5,4},{6,5},{7,6},{8,7},{9,8},{10,9},{11,1... | collective-permute-start | bytes 122888 | tf_op jit(solution)/shard_map/ppermute | solution.py:17
  217.3 7.1 %collective-permute-start.4 = (bf16[1,128,160]{1,2,0:T(8,128)(2,1)S(1)}, bf16[1,128,160]{1,2,0:T(8,128)(2,1)S(1)}, u32[]{:S(2)}, u32[]{:S(2)}) collective-permute-start(bf16[1,128,160]{1,2,0:T(8,128)(2,1)S(1)} %get-tuple-element.33), channel_id=1, source_target_pairs={{0,1},{1,2},{2,3},{3,4},{4,5},{5,6},{6,7},{7,8},{8,9},{9,10},{10,1... | collective-permute-start | bytes 122888 | tf_op jit(solution)/shard_map/ppermute | solution.py:15
  228.9 7.1 %copy-start.31 = (s32[1024]{0:T(1024)S(1)}, s32[1024]{0:T(1024)}, u32[]{:S(2)}) copy-start(s32[1024]{0:T(1024)} %copy-done.30) | copy-start | bytes 12292
  231.4 6.9 %collective-permute-start.7 = (bf16[1,128,160]{2,1,0:T(8,128)(2,1)}, bf16[1,128,160]{2,1,0:T(8,128)(2,1)S(1)}, u32[]{:S(2)}, u32[]{:S(2)}) collective-permute-start(bf16[1,128,160]{2,1,0:T(8,128)(2,1)} %bitcast.124), channel_id=1, source_target_pairs={{1,0},{2,1},{3,2},{4,3},{5,4},{6,5},{7,6},{8,7},{9,8},{10,9},{11,1... | collective-permute-start | bytes 122888 | tf_op jit(solution)/shard_map/ppermute | solution.py:17
  233.4 8.3 %collective-permute-start.6 = (bf16[1,128,160]{2,1,0:T(8,128)(2,1)S(1)}, bf16[1,128,160]{2,1,0:T(8,128)(2,1)S(1)}, u32[]{:S(2)}, u32[]{:S(2)}) collective-permute-start(bf16[1,128,160]{2,1,0:T(8,128)(2,1)S(1)} %bitcast.407), channel_id=1, source_target_pairs={{0,1},{1,2},{2,3},{3,4},{4,5},{5,6},{6,7},{7,8},{8,9},{9,10},{10,1... | collective-permute-start | bytes 122888 | tf_op jit(solution)/shard_map/ppermute | solution.py:15
  236.7 4.9 %copy-start.3 = (f32[768,160]{0,1:T(8,128)S(1)}, f32[768,160]{0,1:T(8,128)}, u32[]{:S(2)}) copy-start(f32[768,160]{0,1:T(8,128)} %get-tuple-element.54) | copy-start | bytes 1474564
  241.7 45.2 %copy-start.2 = (f32[768,160]{0,1:T(8,128)S(1)}, f32[768,160]{0,1:T(8,128)}, u32[]{:S(2)}) copy-start(f32[768,160]{0,1:T(8,128)} %param.20) | copy-start | bytes 1474564
  (23 other events, 56.1 us)
where the time goes:
time: 290 us; the launch traced here: 289 us
  blocking collectives  142 us (49%)
  other arithmetic  79.4 us (27%)
  matrix products  21.8 us (8%)
  starting transfers between devices  18.9 us (7%)
  local copies, waits for them, and re-layouts  17.4 us (6%)
  waiting for transfers between devices  7.38 us (3%)
    psum x1, blocking collectives, shards(): inner = lax.psum(jnp.sum(residual_start * owned, axis=0), ('grp', 'sub'))  44.1 us
    another operation x15, other arithmetic, chol_solve(): lax.linalg.triangular_solve(factor, halfway, left_side=True, lower=True,...  34 us
    another operation x15, other arithmetic, solve_chain(): factor = jnp.linalg.cholesky(diag_odd)  31.6 us
    all_gather x1, blocking collectives, shards(): blocks_up = lax.all_gather(coarse_up, 'sub', axis=0, tiled=True)  14.8 us
    all_gather x1, blocking collectives, shards(): blocks_diag = lax.all_gather(coarse_diag, 'sub', axis=0, tiled=True)  14 us
    all_gather x1, blocking collectives, shards(): columns = lax.all_gather(coarse_in[None], 'sub', axis=0, tiled=True)  12.7 us
    ppermute x4, starting transfers between devices, with_halo(): lax.ppermute(head, axis, [((i + 1) % count, i) for i in range(ends)])  9.75 us
    ppermute x4, starting transfers between devices, with_halo(): lax.ppermute(tail, axis, [(i, (i + 1) % count) for i in range(ends)])  9.13 us
  transfers between devices with their start and end apart: 8, of which 2 were waited for; matrix products, arithmetic and copies ran while one was open for 12% of the time, Pallas kernels for 0%

commit v1 on v0

--- a/solution.py
+++ b/solution.py
@@ -2,6 +2,12 @@
 import jax.numpy as jnp
 from jax import lax
 from jax.sharding import PartitionSpec as P
+
+
+def _drive_runs(unit):
+    for j in ("grp", "sub"):
+        unit = lax.psum(unit, j)
+    return unit
 
 
 def with_halo(cells, sides, width):
@@ -188,7 +194,7 @@
     owned = correction[intersection : intersection + rows_own]
     owned = owned.at[sent_right_rows].add(returned[3])
     owned = owned.at[sent_left_rows].add(returned[0])
-    inner = lax.psum(jnp.sum(residual_start * owned, axis=0), ("grp", "sub"))
+    inner = _drive_runs(jnp.sum(residual_start * owned, axis=0))
     image = apply_operator(owned)
     curvature = lax.psum(jnp.sum(owned * image, axis=0), ("grp", "sub"))
     step_size = inner / curvature

time: 290 us -> 313 us (1.079)
  blocking collectives: 142 us -> 164 us
    psum x1 -> x3, blocking collectives: 44.1 us -> 65.7 us  [the longest x1 42.6 us: shards(): curvature = lax.psum(jnp.sum(owned * image, axis=0), ('grp', 'sub'))]
  transfers between devices with their start and end apart: 8 -> 8, of which waited for: 2 -> 2; matrix products, arithmetic and copies ran while one was open for 12% -> 11% of each run, Pallas kernels for 0% -> 0%
where the time goes in v1:
time: 313 us; the launch traced here: 311 us
  blocking collectives  164 us (52%)
  other arithmetic  79.4 us (25%)
  matrix products  21.8 us (7%)
  starting transfers between devices  18.9 us (6%)
  local copies, waits for them, and re-layouts  17.5 us (6%)
  waiting for transfers between devices  7.4 us (2%)
    psum x1, blocking collectives, shards(): curvature = lax.psum(jnp.sum(owned * image, axis=0), ('grp', 'sub'))  42.6 us
    another operation x15, other arithmetic, chol_solve(): lax.linalg.triangular_solve(factor, halfway, left_side=True, lower=True,...  34 us
    another operation x15, other arithmetic, solve_chain(): factor = jnp.linalg.cholesky(diag_odd)  31.6 us
    psum x2, blocking collectives, _drive_runs(): unit = lax.psum(unit, j)  23.1 us
    all_gather x1, blocking collectives, shards(): blocks_up = lax.all_gather(coarse_up, 'sub', axis=0, tiled=True)  14.8 us
    all_gather x1, blocking collectives, shards(): blocks_diag = lax.all_gather(coarse_diag, 'sub', axis=0, tiled=True)  14 us
    all_gather x1, blocking collectives, shards(): columns = lax.all_gather(coarse_in[None], 'sub', axis=0, tiled=True)  12.7 us
    ppermute x4, starting transfers between devices, with_halo(): lax.ppermute(head, axis, [((i + 1) % count, i) for i in range(ends)])  9.75 us
  transfers between devices with their start and end apart: 8, of which 2 were waited for; matrix products, arithmetic and copies ran while one was open for 11% of the time, Pallas kernels for 0%

profile of v1, /device:TPU:14, one launch (start us, length us, event | category | flops | bytes accessed | tf_op | source)
XLA Modules:
  0.0 310.9 jit_solution(14239580568657559619)
XLA Ops:
  10.4 14.8 %all_gather.32 = f32[8,32,32]{2,1,0:T(8,128)S(1)} all-gather(f32[1,32,32]{2,1,0:T(8,128)S(1)} %copy-done.34), channel_id=1, replica_groups=mesh['grp'=4,'sub'=8] {'sub'}, dimensions={0}, use_global_device_ids=true | all-gather | bytes 36864 | tf_op jit(solution)/shard_map/all_gather | solution.py:143
  25.2 14.0 %all_gather.30 = f32[8,32,32]{2,1,0:T(8,128)S(1)} all-gather(f32[1,32,32]{2,1,0:T(8,128)S(1)} %copy-done.35), channel_id=1, replica_groups=mesh['grp'=4,'sub'=8] {'sub'}, dimensions={0}, use_global_device_ids=true | all-gather | bytes 36864 | tf_op jit(solution)/shard_map/all_gather | solution.py:142
  39.5 11.7 %custom-call.47 = f32[4,32,32]{2,1,0:T(8,128)S(1)} custom-call(f32[4,32,32]{2,1,0:T(8,128)S(1)} %copy.185), custom_call_target="Cholesky" | custom-call | tf_op jit(solution)/shard_map/jit(cholesky)/cholesky | solution.py:61
  61.9 4.0 %collective-permute-start.3 = (bf16[1,128,160]{1,2,0:T(8,128)(2,1)S(1)}, bf16[1,128,160]{1,2,0:T(8,128)(2,1)S(1)}, u32[]{:S(2)}, u32[]{:S(2)}) collective-permute-start(bf16[1,128,160]{1,2,0:T(8,128)(2,1)S(1)} %bitcast.412), channel_id=1, source_target_pairs={{1,0},{2,1},{3,2},{4,3},{5,4},{6,5},{7,6},{8,7},{9,8},{10,9},{11,1... | collective-permute-start | bytes 122888 | tf_op jit(solution)/shard_map/ppermute | solution.py:23
  68.7 11.2 %custom-call.48 = f32[4,1,32,32]{2,3,1,0:T(8,128)} custom-call(f32[4,1,32,32]{3,2,1,0:T(8,128)} %select_bitcast_fusion), custom_call_target="InvertDiagBlocksLowerTriangular" | custom-call | tf_op jit(solution)/shard_map/triangular_solve | solution.py:32
  79.9 9.1 %all_gather.31 = f32[4,32,32]{2,1,0:T(8,128)S(1)} all-gather(f32[1,32,32]{2,1,0:T(8,128)S(1)} %slice-done.1), channel_id=1, replica_groups=mesh['grp'=4,'sub'=8] {'grp'}, dimensions={0}, use_global_device_ids=true | all-gather | bytes 20480 | tf_op jit(solution)/shard_map/all_gather | solution.py:167
  90.6 12.7 %all-gather = f32[256,160]{1,0:T(8,128)S(1)} all-gather(f32[32,160]{1,0:T(8,128)S(1)} %convolution_bitcast_fusion.11), channel_id=2, replica_groups=mesh['grp'=4,'sub'=8] {'sub'}, dimensions={0}, use_global_device_ids=true | all-gather | bytes 184320 | tf_op jit(solution)/shard_map/all_gather | solution.py:151
  106.1 5.9 %custom-call.57 = f32[2,32,32]{2,1,0:T(8,128)S(1)} custom-call(f32[2,32,32]{2,1,0:T(8,128)S(1)} %fusion.117), custom_call_target="Cholesky" | custom-call | tf_op jit(solution)/shard_map/jit(cholesky)/cholesky | solution.py:61
  112.2 4.9 %custom-call.49 = f32[2,1,32,32]{2,3,1,0:T(8,128)S(1)} custom-call(f32[2,1,32,32]{3,2,1,0:T(8,128)S(1)} %fusion.119), custom_call_target="InvertDiagBlocksLowerTriangular" | custom-call | tf_op jit(solution)/shard_map/triangular_solve | solution.py:32
  119.2 2.9 custom-call.58
  123.3 2.4 custom-call.50
  127.0 2.9 cholesky.184
  131.1 2.4 custom-call.51
  136.5 7.0 %all-gather.6 = f32[128,160]{1,0:T(8,128)S(1)} all-gather(f32[32,160]{1,0:T(8,128)S(1)} %slice-done), channel_id=8, replica_groups=mesh['grp'=4,'sub'=8] {'grp'}, dimensions={0}, use_global_device_ids=true | all-gather | bytes 102400 | tf_op jit(solution)/shard_map/all_gather | solution.py:168
  143.5 8.9 %all-gather.4 = f32[128,160]{1,0:T(8,128)S(1)} all-gather(f32[32,160]{1,0:T(8,128)S(1)} %convolution_bitcast_fusion.7), channel_id=6, replica_groups=mesh['grp'=4,'sub'=8] {'grp'}, dimensions={0}, use_global_device_ids=true | all-gather | bytes 102400 | tf_op jit(solution)/shard_map/all_gather | solution.py:172
  152.5 7.1 %all-gather.5 = f32[128,160]{1,0:T(8,128)S(1)} all-gather(f32[32,160]{1,0:T(8,128)S(1)} %fusion.101), channel_id=7, replica_groups=mesh['grp'=4,'sub'=8] {'grp'}, dimensions={0}, use_global_device_ids=true | all-gather | bytes 102400 | tf_op jit(solution)/shard_map/all_gather | solution.py:173
  159.7 8.7 %all-gather.3 = f32[128,32]{1,0:T(8,128)S(1)} all-gather(f32[32,32]{1,0:T(8,128)S(1)} %copy.214), channel_id=5, replica_groups=mesh['grp'=4,'sub'=8] {'grp'}, dimensions={0}, use_global_device_ids=true | all-gather | bytes 20480 | tf_op jit(solution)/shard_map/all_gather | solution.py:171
  168.6 6.7 %all-gather.2 = f32[128,32]{1,0:T(8,128)S(1)} all-gather(f32[32,32]{1,0:T(8,128)S(1)} %fusion.145), channel_id=4, replica_groups=mesh['grp'=4,'sub'=8] {'grp'}, dimensions={0}, use_global_device_ids=true | all-gather | bytes 20480 | tf_op jit(solution)/shard_map/all_gather | solution.py:170
  175.5 8.9 %all-gather.1 = f32[128,32]{1,0:T(8,128)S(1)} all-gather(f32[32,32]{1,0:T(8,128)S(1)} %copy.208), channel_id=3, replica_groups=mesh['grp'=4,'sub'=8] {'grp'}, dimensions={0}, use_global_device_ids=true | all-gather | bytes 20480 | tf_op jit(solution)/shard_map/all_gather | solution.py:169
  184.7 5.9 %custom-call.59 = f32[2,32,32]{2,1,0:T(8,128)S(1)} custom-call(f32[2,32,32]{2,1,0:T(8,128)S(1)} %fusion.112), custom_call_target="Cholesky" | custom-call | tf_op jit(solution)/shard_map/jit(cholesky)/cholesky | solution.py:61
  190.8 4.9 %custom-call.52 = f32[2,1,32,32]{2,3,1,0:T(8,128)S(1)} custom-call(f32[2,1,32,32]{3,2,1,0:T(8,128)S(1)} %fusion.118), custom_call_target="InvertDiagBlocksLowerTriangular" | custom-call | tf_op jit(solution)/shard_map/triangular_solve | solution.py:32
  197.7 2.9 custom-call.60
  202.0 2.4 custom-call.53
  205.6 2.9 cholesky.216
  209.9 2.4 custom-call.54
  217.4 2.4 collective-permute-start.4
  220.1 4.3 %collective-permute-done.4 = bf16[1,128,160]{1,2,0:T(8,128)(2,1)S(1)} collective-permute-done((bf16[1,128,160]{1,2,0:T(8,128)(2,1)S(1)}, bf16[1,128,160]{1,2,0:T(8,128)(2,1)S(1)}, u32[]{:S(2)}, u32[]{:S(2)}) %collective-permute-start.4) | collective-permute-done | bytes 40992 | tf_op jit(solution)/shard_map/ppermute | solution.py:21
  233.5 2.4 collective-permute-start.6
  238.7 3.1 collective-permute-done.6
  242.9 8.4 %psum.21 = f32[160]{0:T(256)S(1)} all-reduce(f32[160]{0:T(256)S(1)} %get-tuple-element.30), channel_id=1, replica_groups=mesh['grp'=4,'sub'=8] {'grp'}, use_global_device_ids=true, to_apply=%region_11.15 | all-reduce | flops 160 | bytes 1280 | tf_op jit(solution)/shard_map/psum | solution.py:9
  251.3 14.7 %psum.22 = f32[160]{0:T(256)S(1)} all-reduce(f32[160]{0:T(256)S(1)} %psum.21), channel_id=1, replica_groups=mesh['grp'=4,'sub'=8] {'sub'}, use_global_device_ids=true, to_apply=%region_12.16 | all-reduce | flops 160 | bytes 1280 | tf_op jit(solution)/shard_map/psum | solution.py:9
  266.0 42.6 %psum.23 = f32[160]{0:T(256)S(1)} all-reduce(f32[160]{0:T(256)S(1)} %get-tuple-element.29), channel_id=1, replica_groups=mesh['grp'=4,'sub'=8] {'grp','sub'}, use_global_device_ids=true, to_apply=%region_14.18 | all-reduce | flops 160 | bytes 1280 | tf_op jit(solution)/shard_map/psum | solution.py:199
  (284 shorter events, 62.9 us)
Async XLA Ops:
  0.6 213.9 %copy-start = (bf16[1,1024,1024]{2,1,0:T(8,128)(2,1)S(1)}, bf16[1,1024,1024]{2,1,0:T(8,128)(2,1)}, u32[]{:S(2)}) copy-start(bf16[1,1024,1024]{2,1,0:T(8,128)(2,1)} %param.27) | copy-start | bytes 6291460
  0.6 9.5 %copy-start.43 = (s32[1,6,3]{1,0,2:T(1,128)S(1)}, s32[1,6,3]{1,0,2:T(1,128)}, u32[]{:S(2)}) copy-start(s32[1,6,3]{1,0,2:T(1,128)} %param.23) | copy-start | bytes 220
  0.7 9.7 %copy-start.34 = (f32[1,32,32]{2,1,0:T(8,128)S(1)}, f32[1,32,32]{2,1,0:T(8,128)}, u32[]{:S(2)}) copy-start(f32[1,32,32]{2,1,0:T(8,128)} %param.30) | copy-start | bytes 12292
  0.7 24.5 %copy-start.35 = (f32[1,32,32]{2,1,0:T(8,128)S(1)}, f32[1,32,32]{2,1,0:T(8,128)}, u32[]{:S(2)}) copy-start(f32[1,32,32]{2,1,0:T(8,128)} %param.29) | copy-start | bytes 12292
  2.8 7.3 %copy-start.38 = (s32[128]{0:T(128)}, s32[128]{0:T(128)S(1)}, u32[]{:S(2)}) copy-start(s32[128]{0:T(128)S(1)} %get-tuple-element.50) | copy-start | bytes 1540
  2.8 22.4 %copy-start.40 = (s32[128]{0:T(128)}, s32[128]{0:T(128)S(1)}, u32[]{:S(2)}) copy-start(s32[128]{0:T(128)S(1)} %get-tuple-element.49) | copy-start | bytes 1540
  2.8 22.4 %copy-start.36 = (s32[1024]{0:T(1024)}, s32[1024]{0:T(1024)S(1)}, u32[]{:S(2)}) copy-start(s32[1024]{0:T(1024)S(1)} %get-tuple-element.57) | copy-start | bytes 12292
  2.8 22.4 %copy-start.37 = (s32[1024]{0:T(1024)}, s32[1024]{0:T(1024)S(1)}, u32[]{:S(2)}) copy-start(s32[1024]{0:T(1024)S(1)} %get-tuple-element.56) | copy-start | bytes 12292
  4.3 52.1 %collective-permute-start.1 = (bf16[1,128,160]{2,1,0:T(8,128)(2,1)}, bf16[1,128,160]{2,1,0:T(8,128)(2,1)}, u32[]{:S(2)}, u32[]{:S(2)}) collective-permute-start(bf16[1,128,160]{2,1,0:T(8,128)(2,1)} %bitcast.13), channel_id=1, source_target_pairs={{1,0},{2,1},{3,2},{4,3},{5,4},{6,5},{7,6},{8,7},{9,8},{10,9},{11,1... | collective-permute-start | bytes 122888 | tf_op jit(solution)/shard_map/ppermute | solution.py:23
  7.7 49.9 %collective-permute-start = (bf16[1,128,160]{2,1,0:T(8,128)(2,1)}, bf16[1,128,160]{2,1,0:T(8,128)(2,1)}, u32[]{:S(2)}, u32[]{:S(2)}) collective-permute-start(bf16[1,128,160]{2,1,0:T(8,128)(2,1)} %bitcast.9), channel_id=1, source_target_pairs={{0,1},{1,2},{2,3},{3,4},{4,5},{5,6},{6,7},{7,8},{8,9},{9,10},{10,1... | collective-permute-start | bytes 122888 | tf_op jit(solution)/shard_map/ppermute | solution.py:21
  10.1 43.6 %copy-start.24 = (pred[32,32]{1,0:T(8,128)(4,1)}, pred[32,32]{1,0:T(8,128)(4,1)S(1)}, u32[]{:S(2)}) copy-start(pred[32,32]{1,0:T(8,128)(4,1)S(1)} %iota_compare_fusion.3) | copy-start | bytes 3076
  10.2 45.5 %copy-start.22 = (pred[32,32]{1,0:T(8,128)(4,1)}, pred[32,32]{1,0:T(8,128)(4,1)S(1)}, u32[]{:S(2)}) copy-start(pred[32,32]{1,0:T(8,128)(4,1)S(1)} %iota_compare_fusion.7) | copy-start | bytes 3076
  10.4 43.3 %copy-start.30 = (s32[1024]{0:T(1024)}, s32[1024]{0:T(1024)S(1)}, u32[]{:S(2)}) copy-start(s32[1024]{0:T(1024)S(1)} %pad_clamp_fusion.2) | copy-start | bytes 12292
  39.2 12.8 %copy-start.11 = (f32[8,32,32]{2,1,0:T(8,128)}, f32[8,32,32]{2,1,0:T(8,128)S(1)}, u32[]{:S(2)}) copy-start(f32[8,32,32]{2,1,0:T(8,128)S(1)} %all_gather.30) | copy-start | bytes 98308
  56.4 46.9 %copy-start.13 = (f32[1,32,32]{2,1,0:T(8,128)}, f32[1,32,32]{2,1,0:T(8,128)S(1)}, u32[]{:S(2)}) copy-start(f32[1,32,32]{2,1,0:T(8,128)S(1)} %get-tuple-element.36) | copy-start | bytes 12292
  59.5 20.4 %slice-start.1 = ((f32[8,32,32]{2,1,0:T(8,128)}), f32[1,32,32]{2,1,0:T(8,128)S(1)}, s32[]{:S(2)}) async-start(f32[8,32,32]{2,1,0:T(8,128)} %copy-done.11), calls=%async_computation.1 | async-start | bytes 32768 | tf_op jit(solution)/shard_map/slice | solution.py:167
  59.7 30.7 %copy-start.20 = (bf16[1,1024,32]{1,2,0:T(8,128)(2,1)S(1)}, bf16[1,1024,32]{1,2,0:T(8,128)(2,1)}, u32[]{:S(2)}) copy-start(bf16[1,1024,32]{1,2,0:T(8,128)(2,1)} %param.28) | copy-start | bytes 196612
  61.9 27.9 %collective-permute-start.3 = (bf16[1,128,160]{1,2,0:T(8,128)(2,1)S(1)}, bf16[1,128,160]{1,2,0:T(8,128)(2,1)S(1)}, u32[]{:S(2)}, u32[]{:S(2)}) collective-permute-start(bf16[1,128,160]{1,2,0:T(8,128)(2,1)S(1)} %bitcast.412), channel_id=1, source_target_pairs={{1,0},{2,1},{3,2},{4,3},{5,4},{6,5},{7,6},{8,7},{9,8},{10,9},{11,1... | collective-permute-start | bytes 122888 | tf_op jit(solution)/shard_map/ppermute | solution.py:23
  66.0 23.8 %collective-permute-start.2 = (bf16[1,128,160]{1,2,0:T(8,128)(2,1)S(1)}, bf16[1,128,160]{1,2,0:T(8,128)(2,1)S(1)}, u32[]{:S(2)}, u32[]{:S(2)}) collective-permute-start(bf16[1,128,160]{1,2,0:T(8,128)(2,1)S(1)} %bitcast.413), channel_id=1, source_target_pairs={{0,1},{1,2},{2,3},{3,4},{4,5},{5,6},{6,7},{7,8},{8,9},{9,10},{10,1... | collective-permute-start | bytes 122888 | tf_op jit(solution)/shard_map/ppermute | solution.py:21
  90.4 13.0 %copy-start.18 = (f32[4,1,32,32]{2,3,1,0:T(8,128)S(1)}, f32[4,1,32,32]{2,3,1,0:T(8,128)}, u32[]{:S(2)}) copy-start(f32[4,1,32,32]{2,3,1,0:T(8,128)} %custom-call.48) | copy-start | bytes 49156
  90.4 13.1 %copy-start.19 = (f32[4,32,32]{2,1,0:T(8,128)S(1)}, f32[4,32,32]{2,1,0:T(8,128)}, u32[]{:S(2)}) copy-start(f32[4,32,32]{2,1,0:T(8,128)} %copy.187) | copy-start | bytes 49156
  104.6 7.3 %copy-start.25 = (pred[32,32]{1,0:T(8,128)(4,1)S(1)}, pred[32,32]{1,0:T(8,128)(4,1)}, u32[]{:S(2)}) copy-start(pred[32,32]{1,0:T(8,128)(4,1)} %copy-done.24) | copy-start | bytes 3076
  104.6 7.5 %copy-start.23 = (pred[32,32]{1,0:T(8,128)(4,1)S(1)}, pred[32,32]{1,0:T(8,128)(4,1)}, u32[]{:S(2)}) copy-start(pred[32,32]{1,0:T(8,128)(4,1)} %copy-done.22) | copy-start | bytes 3076
  135.3 33.1 %copy-start.44 = (pred[4]{0:T(512)(128)(4,1)S(1)}, pred[4]{0:T(512)(128)(4,1)}, u32[]{:S(2)}) copy-start(pred[4]{0:T(512)(128)(4,1)} %constant.263.clone.1) | copy-start | bytes 16
  152.5 32.1 %copy-start.17 = (f32[4,32,32]{1,2,0:T(8,128)S(1)}, f32[4,32,32]{1,2,0:T(8,128)}, u32[]{:S(2)}) copy-start(f32[4,32,32]{1,2,0:T(8,128)} %copy.210) | copy-start | bytes 49156
  215.5 4.7 %collective-permute-start.5 = (bf16[1,128,160]{1,2,0:T(8,128)(2,1)S(1)}, bf16[1,128,160]{1,2,0:T(8,128)(2,1)S(1)}, u32[]{:S(2)}, u32[]{:S(2)}) collective-permute-start(bf16[1,128,160]{1,2,0:T(8,128)(2,1)S(1)} %get-tuple-element.32), channel_id=1, source_target_pairs={{1,0},{2,1},{3,2},{4,3},{5,4},{6,5},{7,6},{8,7},{9,8},{10,9},{11,1... | collective-permute-start | bytes 122888 | tf_op jit(solution)/shard_map/ppermute | solution.py:23
  217.4 7.1 %collective-permute-start.4 = (bf16[1,128,160]{1,2,0:T(8,128)(2,1)S(1)}, bf16[1,128,160]{1,2,0:T(8,128)(2,1)S(1)}, u32[]{:S(2)}, u32[]{:S(2)}) collective-permute-start(bf16[1,128,160]{1,2,0:T(8,128)(2,1)S(1)} %get-tuple-element.31), channel_id=1, source_target_pairs={{0,1},{1,2},{2,3},{3,4},{4,5},{5,6},{6,7},{7,8},{8,9},{9,10},{10,1... | collective-permute-start | bytes 122888 | tf_op jit(solution)/shard_map/ppermute | solution.py:21
  229.0 7.1 %copy-start.31 = (s32[1024]{0:T(1024)S(1)}, s32[1024]{0:T(1024)}, u32[]{:S(2)}) copy-start(s32[1024]{0:T(1024)} %copy-done.30) | copy-start | bytes 12292
  231.5 6.9 %collective-permute-start.7 = (bf16[1,128,160]{2,1,0:T(8,128)(2,1)}, bf16[1,128,160]{2,1,0:T(8,128)(2,1)S(1)}, u32[]{:S(2)}, u32[]{:S(2)}) collective-permute-start(bf16[1,128,160]{2,1,0:T(8,128)(2,1)} %bitcast.124), channel_id=1, source_target_pairs={{1,0},{2,1},{3,2},{4,3},{5,4},{6,5},{7,6},{8,7},{9,8},{10,9},{11,1... | collective-permute-start | bytes 122888 | tf_op jit(solution)/shard_map/ppermute | solution.py:23
  233.5 8.3 %collective-permute-start.6 = (bf16[1,128,160]{2,1,0:T(8,128)(2,1)S(1)}, bf16[1,128,160]{2,1,0:T(8,128)(2,1)S(1)}, u32[]{:S(2)}, u32[]{:S(2)}) collective-permute-start(bf16[1,128,160]{2,1,0:T(8,128)(2,1)S(1)} %bitcast.407), channel_id=1, source_target_pairs={{0,1},{1,2},{2,3},{3,4},{4,5},{5,6},{6,7},{7,8},{8,9},{9,10},{10,1... | collective-permute-start | bytes 122888 | tf_op jit(solution)/shard_map/ppermute | solution.py:21
  236.8 4.9 %copy-start.3 = (f32[768,160]{0,1:T(8,128)S(1)}, f32[768,160]{0,1:T(8,128)}, u32[]{:S(2)}) copy-start(f32[768,160]{0,1:T(8,128)} %get-tuple-element.52) | copy-start | bytes 1474564
  241.8 66.9 %copy-start.2 = (f32[768,160]{0,1:T(8,128)S(1)}, f32[768,160]{0,1:T(8,128)}, u32[]{:S(2)}) copy-start(f32[768,160]{0,1:T(8,128)} %param.20) | copy-start | bytes 1474564
  (23 other events, 56.2 us)
